TPU v7x, 512 devices: a whole 4x4x16 slice. The times are simulated.
512 devices in a mesh: blk: 128 (over z, x, core), grp: 4 (over y).
Axes of the slice: x: 4, y: 4, z: 16, core: 2. Of those that a mesh axis runs over, the one named last changes fastest.
Arguments:
- checkpoint: bfloat16 [131072, 320], P(('blk', 'grp')), may hold values from -4 to 4
- adjoint_rhs: bfloat16 [131072, 320], P(('blk', 'grp')), may hold values from -6 to 6
- new_position: int32 [131072], P(('blk', 'grp')), may hold values from 0 to 131071, as said below
- old_position: int32 [131072], P(('blk', 'grp')), may hold values from 0 to 131071, as said below
- left_matrix: bfloat16 [320, 320], replicated, may hold values from -0.3125 to 0.3125
- right_matrix: bfloat16 [320, 320], replicated, may hold values from -0.3125 to 0.3125
- face_block: int32 [6, 131072], P(None, ('blk', 'grp')), may hold values from -1 to 131071, as said below
- face_weight: float32 [6, 131072], P(None, ('blk', 'grp')), may hold values from 0.3 to 0.9
- donor_block: int32 [2, 131072], P(None, ('blk', 'grp')), may hold values from 0 to 131071, as said below
- donor_weight: float32 [2, 131072], P(None, ('blk', 'grp')), may hold values from 0.2 to 0.7
Outputs:
- adjoint: float32 [131072, 320], P(('blk', 'grp'))
Inputs may be any that keep to these rules, and one draw needn't show every extreme that they name: `new_position`: A permutation of the block indices that keeps each block's index along grp; the blocks of one device go to 64 devices along blk, exactly 4 blocks to each of them. `old_position`: the inverse permutation of new_position. `face_block`: each entry is -1 or a block of the same grp index whose place in that group's order of blocks (blk index times 256 plus the local index) lies within 256 places of the block's own, taken cyclically. `donor_block`: each donor lies on the device of the same blk index and another grp index, among the first 128 blocks of that device in the new order.
All inputs are finite; a program needn't handle non-finite values.
Results may differ from a plain program's by a relative error of at most 0.0014.
Values may be sent and summed in bfloat16 or wider, within the bound.
A program may use at most 64 MiB of HBM per device.

v0:
```python
import jax
import jax.numpy as jnp
from jax import lax
from jax.sharding import PartitionSpec as P


def passed_along(block, axis, distance):
    devices = range(lax.axis_size(axis))
    route = [((i - distance) % len(devices), i) for i in devices]
    return lax.ppermute(block, axis, route)


def coefficients(state):
    values = state.astype(jnp.float32)
    left_gain = 0.5 * jnp.tanh(values)
    right_gain = 0.4 * jnp.tanh(1.5 * values - 0.5)
    dual_diag = 2.0 + values * values
    return (left_gain, right_gain, dual_diag)


def transposed_apply(
    adjoint, left_gain, right_gain, left_matrix, right_matrix, left_trans, right_trans
):
    rounded = adjoint.astype(jnp.bfloat16)
    first_proj = jnp.dot(rounded, left_matrix, preferred_element_type=jnp.float32)
    second_proj = jnp.dot(rounded, right_trans, preferred_element_type=jnp.float32)
    first_mid = (first_proj * left_gain).astype(jnp.bfloat16)
    second_mid = (second_proj * right_gain).astype(jnp.bfloat16)
    return jnp.dot(first_mid, right_matrix, preferred_element_type=jnp.float32) + jnp.dot(
        second_mid, left_trans, preferred_element_type=jnp.float32
    )


def face_sum(block_pool, face_index, face_valid, face_weight):
    row_count = face_index.shape[1]
    total_face = jnp.zeros((row_count, block_pool.shape[1]), jnp.float32)
    for face_id in range(face_index.shape[0]):
        fetched = jnp.take(block_pool, face_index[face_id], axis=0).reshape(row_count, 5, 4, 4, 4)
        cell_axis = 2 + face_id // 2
        from_cell = 3 if face_id % 2 == 0 else 0
        face_slab = lax.slice_in_dim(fetched, from_cell, from_cell + 1, axis=cell_axis)
        scale_face = jnp.where(face_valid[face_id], face_weight[face_id], 0.0)
        face_slab = face_slab * scale_face.reshape(row_count, 1, 1, 1, 1)
        pad_shape = list(face_slab.shape)
        pad_shape[cell_axis] = 3
        padding = jnp.zeros(pad_shape, jnp.float32)
        if face_id % 2 == 0:
            placed = jnp.concatenate([face_slab, padding], axis=cell_axis)
        else:
            placed = jnp.concatenate([padding, face_slab], axis=cell_axis)
        total_face = total_face + placed.reshape(row_count, block_pool.shape[1])
    return total_face


def fringe_sum(block_pool, donor_index, donor_weight):
    total_fringe = jnp.zeros((donor_index.shape[1], block_pool.shape[1]), jnp.float32)
    for donor_id in range(donor_index.shape[0]):
        fetched = jnp.take(block_pool, donor_index[donor_id], axis=0)
        total_fringe = total_fringe + donor_weight[donor_id][:, None] * fetched
    return total_fringe


def body(
    checkpoint,
    adjoint_rhs,
    new_position,
    old_position,
    left_matrix,
    right_matrix,
    face_block,
    face_weight,
    donor_block,
    donor_weight,
):
    blk_count = lax.axis_size("blk")
    grp_count = lax.axis_size("grp")
    per_device = checkpoint.shape[0]
    capacity = max(2, 2 * per_device // blk_count)
    my_blk = lax.axis_index("blk")
    left_trans = left_matrix.T
    right_trans = right_matrix.T
    target = new_position // per_device // grp_count
    positions = jnp.arange(per_device, dtype=jnp.int32)
    send_rank = jnp.sum(
        (target[:, None] == target[None, :]) & (positions[None, :] < positions[:, None]), axis=1
    )
    send_slot = target * capacity + send_rank
    anchor = old_position // per_device // grp_count
    anchor_local = old_position % per_device
    recv_rank = jnp.sum(
        (anchor[:, None] == anchor[None, :]) & (anchor_local[None, :] < anchor_local[:, None]),
        axis=1,
    )
    recv_slot = anchor * capacity + recv_rank
    face_valid = face_block >= 0
    face_blk = face_block // per_device // grp_count
    face_place = (face_blk - my_blk + 1) % blk_count * per_device + face_block % per_device
    face_local = jnp.where(face_valid, face_place, 0)
    donor_grp = donor_block // per_device % grp_count
    donor_within = donor_block % per_device

    def pack_rows(values, slot_ids):
        buffer = (
            jnp.zeros((blk_count * capacity, values.shape[1]), values.dtype)
            .at[slot_ids]
            .set(values)
        )
        return buffer.reshape(blk_count, capacity, values.shape[1])

    def unpack_rows(received, slot_ids):
        return received.reshape(blk_count * capacity, received.shape[2])[slot_ids]

    got_state, got_rhs = (
        lax.all_to_all(
            pack_rows(checkpoint, send_slot), "blk", split_axis=0, concat_axis=0, tiled=True
        ),
        lax.all_to_all(
            pack_rows(adjoint_rhs, send_slot), "blk", split_axis=0, concat_axis=0, tiled=True
        ),
    )
    state_new = unpack_rows(got_state, recv_slot)
    rhs_float = unpack_rows(got_rhs, recv_slot).astype(jnp.float32)
    left_gain, right_gain, dual_diag = coefficients(state_new)
    result = rhs_float / dual_diag
    for sweep_step in range(2):
        applied = transposed_apply(
            result, left_gain, right_gain, left_matrix, right_matrix, left_trans, right_trans
        )
        below_adj = passed_along(result.astype(jnp.bfloat16), "blk", 1).astype(result.dtype)
        above_adj = passed_along(result.astype(jnp.bfloat16), "blk", -1).astype(result.dtype)
        block_pool = jnp.concatenate([below_adj, result, above_adj], axis=0)
        face_term = face_sum(block_pool, face_local, face_valid, face_weight)
        group_pool = lax.all_gather(result, "grp", axis=0, tiled=True)
        donor_local = donor_grp * per_device + donor_within
        fringe_term = fringe_sum(group_pool, donor_local, donor_weight)
        face_term, fringe_term = (face_term, fringe_term)
        result = (rhs_float - applied - face_term - fringe_term) / dual_diag
    return result


def solution(mesh):
    in_specs = (
        P(("blk", "grp"), None),
        P(("blk", "grp"), None),
        P(("blk", "grp")),
        P(("blk", "grp")),
        P(),
        P(),
        P(None, ("blk", "grp")),
        P(None, ("blk", "grp")),
        P(None, ("blk", "grp")),
        P(None, ("blk", "grp")),
    )
    out_specs = P(("blk", "grp"), None)
    return jax.shard_map(body, mesh=mesh, in_specs=in_specs, out_specs=out_specs, check_vma=False)
```

profile of v0, /device:TPU:2, one launch (start us, length us, event | category | flops | bytes accessed | tf_op | source)
XLA Modules:
  0.0 188.3 jit_solution(17737311999590870322)
XLA Ops:
  9.3 1.6 scatter_custom_fusion.1
  11.7 19.6 %all-to-all-start.1 = ((bf16[128,4,320]{2,1,0:T(4,128)(2,1)}), bf16[128,4,320]{2,1,0:T(4,128)(2,1)S(1)}, u32[]{:S(2)}, u32[]{:S(2)}) async-start(bf16[128,4,320]{2,1,0:T(4,128)(2,1)} %reshape.182), calls=%async_computation.1 | async-start | bytes 786432 | tf_op jit(solution)/shard_map/all_to_all | solution.py:114
  31.8 1.6 scatter_custom_fusion
  34.7 22.8 %all-to-all-done.1 = bf16[128,4,320]{2,1,0:T(4,128)(2,1)S(1)} async-done(((bf16[128,4,320]{2,1,0:T(4,128)(2,1)}), bf16[128,4,320]{2,1,0:T(4,128)(2,1)S(1)}, u32[]{:S(2)}, u32[]{:S(2)}) %all-to-all-start.1) | async-done | bytes 327712 | tf_op jit(solution)/shard_map/all_to_all | solution.py:114
  57.6 8.0 %all-to-all-start = ((bf16[128,4,320]{2,1,0:T(4,128)(2,1)}), bf16[128,4,320]{2,1,0:T(4,128)(2,1)S(1)}, u32[]{:S(2)}, u32[]{:S(2)}) async-start(bf16[128,4,320]{2,1,0:T(4,128)(2,1)} %reshape.180), calls=%async_computation | async-start | bytes 786432 | tf_op jit(solution)/shard_map/all_to_all | solution.py:117
  66.1 1.2 gather_fusion.1
  67.4 24.5 %all-to-all-done = bf16[128,4,320]{2,1,0:T(4,128)(2,1)S(1)} async-done(((bf16[128,4,320]{2,1,0:T(4,128)(2,1)}), bf16[128,4,320]{2,1,0:T(4,128)(2,1)S(1)}, u32[]{:S(2)}, u32[]{:S(2)}) %all-to-all-start) | async-done | bytes 327712 | tf_op jit(solution)/shard_map/all_to_all | solution.py:117
  92.1 1.2 gather_fusion
  94.2 2.9 %collective-permute-start = (bf16[256,320]{0,1:T(8,128)(2,1)S(1)}, bf16[256,320]{0,1:T(8,128)(2,1)S(1)}, u32[]{:S(2)}, u32[]{:S(2)}) collective-permute-start(bf16[256,320]{0,1:T(8,128)(2,1)S(1)} %get-tuple-element.8), channel_id=1, source_target_pairs={{508,0},{0,4},{4,8},{8,12},{12,16},{16,20},{20,24},{24,28},{28,32}... | collective-permute-start | bytes 491528 | tf_op jit(solution)/shard_map/ppermute | solution.py:10
  97.1 2.7 %collective-permute-start.1 = (bf16[256,320]{0,1:T(8,128)(2,1)S(1)}, bf16[256,320]{0,1:T(8,128)(2,1)S(1)}, u32[]{:S(2)}, u32[]{:S(2)}) collective-permute-start(bf16[256,320]{0,1:T(8,128)(2,1)S(1)} %get-tuple-element.8), channel_id=1, source_target_pairs={{4,0},{8,4},{12,8},{16,12},{20,16},{24,20},{28,24},{32,28},{36,32}... | collective-permute-start | bytes 491528 | tf_op jit(solution)/shard_map/ppermute | solution.py:10
  100.0 1.4 fusion.13
  101.4 1.1 collective-permute-done.1
  114.5 1.1 slice_multiply_fusion.6
  116.0 12.3 %all-gather.3.cloned.1.call-done = f32[1024,320]{0,1:T(8,128)} async-done(((f32[256,320]{0,1:T(8,128)}), f32[1024,320]{0,1:T(8,128)}) %all-gather.3.cloned.1.call-update) | async-done | bytes 1310736 | tf_op jit(solution)/shard_map/all_gather | solution.py:133
  128.3 1.8 copy.97
  132.5 2.5 %fusion.66 = (bf16[256,320]{0,1:T(8,128)(2,1)S(1)}, f32[256,320]{0,1:T(8,128)}) fusion(bf16[256,320]{0,1:T(8,128)(2,1)S(1)} %copy.84, f32[256,320]{0,1:T(8,128)S(1)} %copy.100, pred[256]{0:T(512)(128)(4,1)S(1)} %get-tuple-element.35, f32[256]{0:T(256)S(1)} %bitcast.84, f32[256,320]{0,1:T(8,128)S(1)} %copy.98, pred[256]{0:T(512)(128)(4,1)S(1)} %get-tuple-element.36, ...), kind=kOutput, calls=%fused_computation.198 | convolution fusion | flops 107069440 | bytes 2542080 | tf_op jit(solution)/shard_map/dot_general | solution.py:29
  135.0 1.9 %collective-permute-start.2 = (bf16[256,320]{0,1:T(8,128)(2,1)S(1)}, bf16[256,320]{0,1:T(8,128)(2,1)S(1)}, u32[]{:S(2)}, u32[]{:S(2)}) collective-permute-start(bf16[256,320]{0,1:T(8,128)(2,1)S(1)} %get-tuple-element.27), channel_id=1, source_target_pairs={{508,0},{0,4},{4,8},{8,12},{12,16},{16,20},{20,24},{24,28},{28,32}... | collective-permute-start | bytes 491528 | tf_op jit(solution)/shard_map/ppermute | solution.py:10
  136.9 3.9 %collective-permute-start.3 = (bf16[256,320]{0,1:T(8,128)(2,1)S(1)}, bf16[256,320]{0,1:T(8,128)(2,1)S(1)}, u32[]{:S(2)}, u32[]{:S(2)}) collective-permute-start(bf16[256,320]{0,1:T(8,128)(2,1)S(1)} %get-tuple-element.27), channel_id=1, source_target_pairs={{4,0},{8,4},{12,8},{16,12},{20,16},{24,20},{28,24},{32,28},{36,32}... | collective-permute-start | bytes 491528 | tf_op jit(solution)/shard_map/ppermute | solution.py:10
  140.8 1.4 fusion.12
  142.2 1.1 collective-permute-done.3
  143.8 1.9 gather_fusion.14
  145.7 1.1 gather_fusion.13
  146.8 1.1 gather_fusion.12
  147.9 1.1 gather_fusion.11
  149.1 1.1 gather_fusion.10
  150.2 1.1 gather_fusion.15
  151.3 1.1 broadcast_select_fusion.1
  156.4 18.4 %all-gather.5.cloned.1.call-done = f32[1024,320]{0,1:T(8,128)} async-done(((f32[256,320]{0,1:T(8,128)}), f32[1024,320]{0,1:T(8,128)}) %all-gather.5.cloned.1.call-update) | async-done | bytes 1310736 | tf_op jit(solution)/shard_map/all_gather | solution.py:133
  174.9 1.8 copy.113
  176.7 1.1 gather_fusion.16
  177.8 1.1 gather_fusion.17
  180.1 1.3 fusion.7
  (231 shorter events, 26.5 us)
Async XLA Ops:
  6.5 93.5 %copy-start = (bf16[320,320]{1,0:T(8,128)(2,1)S(1)}, bf16[320,320]{1,0:T(8,128)(2,1)}, u32[]{:S(2)}) copy-start(bf16[320,320]{1,0:T(8,128)(2,1)} %param.19) | copy-start | bytes 614404
  11.7 45.8 %all-to-all-start.1 = ((bf16[128,4,320]{2,1,0:T(4,128)(2,1)}), bf16[128,4,320]{2,1,0:T(4,128)(2,1)S(1)}, u32[]{:S(2)}, u32[]{:S(2)}) async-start(bf16[128,4,320]{2,1,0:T(4,128)(2,1)} %reshape.182), calls=%async_computation.1 | async-start | bytes 786432 | tf_op jit(solution)/shard_map/all_to_all | solution.py:114
  34.3 68.7 %copy-start.27 = (s32[1024]{0:T(1024)}, s32[1024]{0:T(1024)S(1)}, u32[]{:S(2)}) copy-start(s32[1024]{0:T(1024)S(1)} %pad_clamp_fusion.7) | copy-start | bytes 12292
  34.4 70.1 %copy-start.28 = (s32[1024]{0:T(1024)}, s32[1024]{0:T(1024)S(1)}, u32[]{:S(2)}) copy-start(s32[1024]{0:T(1024)S(1)} %pad_clamp_fusion.6) | copy-start | bytes 12292
  34.4 71.4 %copy-start.29 = (s32[1024]{0:T(1024)}, s32[1024]{0:T(1024)S(1)}, u32[]{:S(2)}) copy-start(s32[1024]{0:T(1024)S(1)} %pad_clamp_fusion.5) | copy-start | bytes 12292
  34.4 73.4 %copy-start.31 = (s32[1024]{0:T(1024)}, s32[1024]{0:T(1024)S(1)}, u32[]{:S(2)}) copy-start(s32[1024]{0:T(1024)S(1)} %pad_clamp_fusion.4) | copy-start | bytes 12292
  34.5 75.5 %copy-start.32 = (s32[1024]{0:T(1024)}, s32[1024]{0:T(1024)S(1)}, u32[]{:S(2)}) copy-start(s32[1024]{0:T(1024)S(1)} %pad_clamp_fusion.3) | copy-start | bytes 12292
  34.5 77.5 %copy-start.30 = (s32[1024]{0:T(1024)}, s32[1024]{0:T(1024)S(1)}, u32[]{:S(2)}) copy-start(s32[1024]{0:T(1024)S(1)} %pad_clamp_fusion.2) | copy-start | bytes 12292
  34.6 95.5 %copy-start.25 = (s32[1024]{0:T(1024)}, s32[1024]{0:T(1024)S(1)}, u32[]{:S(2)}) copy-start(s32[1024]{0:T(1024)S(1)} %pad_clamp_fusion) | copy-start | bytes 12292
  34.6 96.6 %copy-start.26 = (s32[1024]{0:T(1024)}, s32[1024]{0:T(1024)S(1)}, u32[]{:S(2)}) copy-start(s32[1024]{0:T(1024)S(1)} %pad_clamp_fusion.1) | copy-start | bytes 12292
  34.7 69.4 %copy-start.36 = (pred[256]{0:T(512)(128)(4,1)}, pred[256]{0:T(512)(128)(4,1)S(1)}, u32[]{:S(2)}) copy-start(pred[256]{0:T(512)(128)(4,1)S(1)} %compare_and_fusion.7) | copy-start | bytes 772
  34.7 70.7 %copy-start.38 = (pred[256]{0:T(512)(128)(4,1)}, pred[256]{0:T(512)(128)(4,1)S(1)}, u32[]{:S(2)}) copy-start(pred[256]{0:T(512)(128)(4,1)S(1)} %compare_and_fusion.6) | copy-start | bytes 772
  34.7 72.1 %copy-start.42 = (pred[256]{0:T(512)(128)(4,1)}, pred[256]{0:T(512)(128)(4,1)S(1)}, u32[]{:S(2)}) copy-start(pred[256]{0:T(512)(128)(4,1)S(1)} %compare_and_fusion.5) | copy-start | bytes 772
  34.7 74.1 %copy-start.44 = (pred[256]{0:T(512)(128)(4,1)}, pred[256]{0:T(512)(128)(4,1)S(1)}, u32[]{:S(2)}) copy-start(pred[256]{0:T(512)(128)(4,1)S(1)} %compare_and_fusion.4) | copy-start | bytes 772
  57.6 34.3 %all-to-all-start = ((bf16[128,4,320]{2,1,0:T(4,128)(2,1)}), bf16[128,4,320]{2,1,0:T(4,128)(2,1)S(1)}, u32[]{:S(2)}, u32[]{:S(2)}) async-start(bf16[128,4,320]{2,1,0:T(4,128)(2,1)} %reshape.180), calls=%async_computation | async-start | bytes 786432 | tf_op jit(solution)/shard_map/all_to_all | solution.py:117
  65.6 62.7 %all-gather.3.cloned.1.call-start = ((), (), s32[]{:S(2)}) async-start(), calls=%async_computation.2 | async-start | bytes 1638400 | tf_op jit(solution)/shard_map/all_gather | solution.py:133
  65.7 47.4 %copy-start.40 = (pred[256]{0:T(512)(128)(4,1)}, pred[256]{0:T(512)(128)(4,1)S(1)}, u32[]{:S(2)}) copy-start(pred[256]{0:T(512)(128)(4,1)S(1)} %compare_and_fusion.2) | copy-start | bytes 772
  65.7 66.7 %copy-start.52 = (pred[256]{0:T(512)(128)(4,1)}, pred[256]{0:T(512)(128)(4,1)S(1)}, u32[]{:S(2)}) copy-start(pred[256]{0:T(512)(128)(4,1)S(1)} %get-tuple-element.35) | copy-start | bytes 772
  65.7 66.7 %copy-start.54 = (pred[256]{0:T(512)(128)(4,1)}, pred[256]{0:T(512)(128)(4,1)S(1)}, u32[]{:S(2)}) copy-start(pred[256]{0:T(512)(128)(4,1)S(1)} %get-tuple-element.36) | copy-start | bytes 772
  65.8 66.6 %copy-start.48 = (f32[1,256]{1,0:T(1,128)}, f32[1,256]{1,0:T(1,128)S(1)}, u32[]{:S(2)}) copy-start(f32[1,256]{1,0:T(1,128)S(1)} %get-tuple-element.21) | copy-start | bytes 3076
  65.8 66.6 %copy-start.50 = (f32[1,256]{1,0:T(1,128)}, f32[1,256]{1,0:T(1,128)S(1)}, u32[]{:S(2)}) copy-start(f32[1,256]{1,0:T(1,128)S(1)} %get-tuple-element.22) | copy-start | bytes 3076
  65.8 47.6 %copy-start.17 = (f32[1,256]{1,0:T(1,128)}, f32[1,256]{1,0:T(1,128)S(1)}, u32[]{:S(2)}) copy-start(f32[1,256]{1,0:T(1,128)S(1)} %get-tuple-element.9) | copy-start | bytes 3076
  65.8 47.6 %copy-start.19 = (f32[1,256]{1,0:T(1,128)}, f32[1,256]{1,0:T(1,128)S(1)}, u32[]{:S(2)}) copy-start(f32[1,256]{1,0:T(1,128)S(1)} %get-tuple-element.13) | copy-start | bytes 3076
  65.9 47.6 %copy-start.21 = (f32[1,256]{1,0:T(1,128)}, f32[1,256]{1,0:T(1,128)S(1)}, u32[]{:S(2)}) copy-start(f32[1,256]{1,0:T(1,128)S(1)} %get-tuple-element.12) | copy-start | bytes 3076
  65.9 47.6 %copy-start.23 = (f32[1,256]{1,0:T(1,128)}, f32[1,256]{1,0:T(1,128)S(1)}, u32[]{:S(2)}) copy-start(f32[1,256]{1,0:T(1,128)S(1)} %get-tuple-element.11) | copy-start | bytes 3076
  65.9 48.6 %copy-start.13 = (f32[1,256]{1,0:T(1,128)}, f32[1,256]{1,0:T(1,128)S(1)}, u32[]{:S(2)}) copy-start(f32[1,256]{1,0:T(1,128)S(1)} %get-tuple-element.14) | copy-start | bytes 3076
  65.9 48.6 %copy-start.15 = (f32[1,256]{1,0:T(1,128)}, f32[1,256]{1,0:T(1,128)S(1)}, u32[]{:S(2)}) copy-start(f32[1,256]{1,0:T(1,128)S(1)} %get-tuple-element.10) | copy-start | bytes 3076
  94.2 7.2 %collective-permute-start = (bf16[256,320]{0,1:T(8,128)(2,1)S(1)}, bf16[256,320]{0,1:T(8,128)(2,1)S(1)}, u32[]{:S(2)}, u32[]{:S(2)}) collective-permute-start(bf16[256,320]{0,1:T(8,128)(2,1)S(1)} %get-tuple-element.8), channel_id=1, source_target_pairs={{508,0},{0,4},{4,8},{8,12},{12,16},{16,20},{20,24},{24,28},{28,32}... | collective-permute-start | bytes 491528 | tf_op jit(solution)/shard_map/ppermute | solution.py:10
  97.1 5.5 %collective-permute-start.1 = (bf16[256,320]{0,1:T(8,128)(2,1)S(1)}, bf16[256,320]{0,1:T(8,128)(2,1)S(1)}, u32[]{:S(2)}, u32[]{:S(2)}) collective-permute-start(bf16[256,320]{0,1:T(8,128)(2,1)S(1)} %get-tuple-element.8), channel_id=1, source_target_pairs={{4,0},{8,4},{12,8},{16,12},{20,16},{24,20},{28,24},{32,28},{36,32}... | collective-permute-start | bytes 491528 | tf_op jit(solution)/shard_map/ppermute | solution.py:10
  99.8 75.1 %all-gather.5.cloned.1.call-start = ((), (), s32[]{:S(2)}) async-start(), calls=%async_computation.3 | async-start | bytes 1638400 | tf_op jit(solution)/shard_map/all_gather | solution.py:133
  135.0 7.2 %collective-permute-start.2 = (bf16[256,320]{0,1:T(8,128)(2,1)S(1)}, bf16[256,320]{0,1:T(8,128)(2,1)S(1)}, u32[]{:S(2)}, u32[]{:S(2)}) collective-permute-start(bf16[256,320]{0,1:T(8,128)(2,1)S(1)} %get-tuple-element.27), channel_id=1, source_target_pairs={{508,0},{0,4},{4,8},{8,12},{12,16},{16,20},{20,24},{24,28},{28,32}... | collective-permute-start | bytes 491528 | tf_op jit(solution)/shard_map/ppermute | solution.py:10
  136.9 6.5 %collective-permute-start.3 = (bf16[256,320]{0,1:T(8,128)(2,1)S(1)}, bf16[256,320]{0,1:T(8,128)(2,1)S(1)}, u32[]{:S(2)}, u32[]{:S(2)}) collective-permute-start(bf16[256,320]{0,1:T(8,128)(2,1)S(1)} %get-tuple-element.27), channel_id=1, source_target_pairs={{4,0},{8,4},{12,8},{16,12},{20,16},{24,20},{28,24},{32,28},{36,32}... | collective-permute-start | bytes 491528 | tf_op jit(solution)/shard_map/ppermute | solution.py:10
  (32 other events, 293.7 us)
Sparse Core Ops, SparseCore 0:
  99.9 28.3 all-gather.2
  140.9 33.9 all-gather.4
where the time goes:
time: 189 us; the launch traced here: 188 us
  waiting for transfers between devices  80.4 us (43%)
  local copies, waits for them, and re-layouts  39.3 us (21%)
  starting transfers between devices  39.2 us (21%)
  between operations  14.9 us (8%)
  other arithmetic  8.04 us (4%)
  matrix products  6.58 us (3%)
    all_gather x2, waiting for transfers between devices, body(): group_pool = lax.all_gather(result, 'grp', axis=0, tiled=True)  30.8 us
    all_to_all x1, waiting for transfers between devices, body(): lax.all_to_all(pack_rows(adjoint_rhs, send_slot), 'blk', split_axis=0, co...  24.5 us
    all_to_all x1, waiting for transfers between devices, body(): lax.all_to_all(pack_rows(checkpoint, send_slot), 'blk', split_axis=0, con...  22.8 us
    all_to_all x1, starting transfers between devices, body(): lax.all_to_all(pack_rows(checkpoint, send_slot), 'blk', split_axis=0, con...  19.6 us
    gather x12, local copies, waits for them, and re-layouts, face_sum(): jnp.take(block_pool, face_index[face_id], axis=0)  13.4 us
    ppermute x4, starting transfers between devices, passed_along(): return lax.ppermute(block, axis, route)  11.3 us
    all_to_all x1, starting transfers between devices, body(): lax.all_to_all(pack_rows(adjoint_rhs, send_slot), 'blk', split_axis=0, co...  8.05 us
    gather x8, local copies, waits for them, and re-layouts, fringe_sum(): fetched = jnp.take(block_pool, donor_index[donor_id], axis=0)  4.8 us
  transfers between devices with their start and end apart: 8, of which 6 were waited for; matrix products, arithmetic and copies ran while one was open for 17% of the time, Pallas kernels for 0%

commit v1 on v0

--- a/solution.py
+++ b/solution.py
@@ -130,7 +130,9 @@
         above_adj = passed_along(result.astype(jnp.bfloat16), "blk", -1).astype(result.dtype)
         block_pool = jnp.concatenate([below_adj, result, above_adj], axis=0)
         face_term = face_sum(block_pool, face_local, face_valid, face_weight)
-        group_pool = lax.all_gather(result, "grp", axis=0, tiled=True)
+        group_pool = jnp.concatenate(
+            lax.all_to_all(jnp.stack([result] * lax.axis_size("grp")), "grp", 0, 0), axis=0
+        )
         donor_local = donor_grp * per_device + donor_within
         fringe_term = fringe_sum(group_pool, donor_local, donor_weight)
         face_term, fringe_term = (face_term, fringe_term)

time: 189 us -> 170 us (0.90)
  the two profiles are of different devices: /device:TPU:2 before, /device:TPU:8 now
where the time goes in v1:
time: 170 us; the launch traced here: 169 us
  starting transfers between devices  56.2 us (33%)
  local copies, waits for them, and re-layouts  48.5 us (29%)
  waiting for transfers between devices  38.6 us (23%)
  other arithmetic  19.1 us (11%)
  matrix products  5.66 us (3%)
    all_to_all x1, waiting for transfers between devices, body(): lax.all_to_all(pack_rows(adjoint_rhs, send_slot), 'blk', split_axis=0, co...  21.9 us
    all_to_all x1, starting transfers between devices, body(): lax.all_to_all(pack_rows(checkpoint, send_slot), 'blk', split_axis=0, con...  19.9 us
    ppermute x4, starting transfers between devices, passed_along(): return lax.ppermute(block, axis, route)  17.8 us
    gather x12, local copies, waits for them, and re-layouts, face_sum(): jnp.take(block_pool, face_index[face_id], axis=0)  16.9 us
    all_to_all x1, waiting for transfers between devices, body(): lax.all_to_all(pack_rows(checkpoint, send_slot), 'blk', split_axis=0, con...  16.7 us
    all_to_all x2, starting transfers between devices, body(): lax.all_to_all(jnp.stack([result] * lax.axis_size('grp')), 'grp', 0, 0)  9.84 us
    all_to_all x1, starting transfers between devices, body(): lax.all_to_all(pack_rows(adjoint_rhs, send_slot), 'blk', split_axis=0, co...  8.71 us
    reshape x12, local copies, waits for them, and re-layouts, face_sum(): jnp.take(block_pool, face_index[face_id], axis=0)  5.47 us
  transfers between devices with their start and end apart: 8, of which 2 were waited for; matrix products, arithmetic and copies ran while one was open for 33% of the time, Pallas kernels for 0%

profile of v1, /device:TPU:8, one launch (start us, length us, event | category | flops | bytes accessed | tf_op | source)
XLA Modules:
  0.0 169.2 jit_solution(15859565760449419995)
XLA Ops:
  2.7 1.6 scatter_custom_fusion.1
  5.2 19.9 %all-to-all-start.1 = ((bf16[128,4,320]{2,1,0:T(4,128)(2,1)}), bf16[128,4,320]{2,1,0:T(4,128)(2,1)S(1)}, u32[]{:S(2)}, u32[]{:S(2)}) async-start(bf16[128,4,320]{2,1,0:T(4,128)(2,1)} %reshape.193), calls=%async_computation.1 | async-start | bytes 786432 | tf_op jit(solution)/shard_map/all_to_all | solution.py:114
  25.6 1.6 scatter_custom_fusion
  34.1 16.7 %all-to-all-done.1 = bf16[128,4,320]{2,1,0:T(4,128)(2,1)S(1)} async-done(((bf16[128,4,320]{2,1,0:T(4,128)(2,1)}), bf16[128,4,320]{2,1,0:T(4,128)(2,1)S(1)}, u32[]{:S(2)}, u32[]{:S(2)}) %all-to-all-start.1) | async-done | bytes 327712 | tf_op jit(solution)/shard_map/all_to_all | solution.py:114
  50.8 8.7 %all-to-all-start = ((bf16[128,4,320]{2,1,0:T(4,128)(2,1)}), bf16[128,4,320]{2,1,0:T(4,128)(2,1)S(1)}, u32[]{:S(2)}, u32[]{:S(2)}) async-start(bf16[128,4,320]{2,1,0:T(4,128)(2,1)} %reshape.191), calls=%async_computation | async-start | bytes 786432 | tf_op jit(solution)/shard_map/all_to_all | solution.py:117
  61.9 1.2 gather_fusion.1
  63.2 21.9 %all-to-all-done = bf16[128,4,320]{2,1,0:T(4,128)(2,1)S(1)} async-done(((bf16[128,4,320]{2,1,0:T(4,128)(2,1)}), bf16[128,4,320]{2,1,0:T(4,128)(2,1)S(1)}, u32[]{:S(2)}, u32[]{:S(2)}) %all-to-all-start) | async-done | bytes 327712 | tf_op jit(solution)/shard_map/all_to_all | solution.py:117
  85.3 1.2 gather_fusion
  86.7 1.9 %collective-permute-start = (bf16[256,320]{0,1:T(8,128)(2,1)S(1)}, bf16[256,320]{0,1:T(8,128)(2,1)S(1)}, u32[]{:S(2)}, u32[]{:S(2)}) collective-permute-start(bf16[256,320]{0,1:T(8,128)(2,1)S(1)} %get-tuple-element.8), channel_id=1, source_target_pairs={{508,0},{0,4},{4,8},{8,12},{12,16},{16,20},{20,24},{24,28},{28,32}... | collective-permute-start | bytes 491528 | tf_op jit(solution)/shard_map/ppermute | solution.py:10
  88.6 7.0 %collective-permute-start.1 = (bf16[256,320]{0,1:T(8,128)(2,1)S(1)}, bf16[256,320]{0,1:T(8,128)(2,1)S(1)}, u32[]{:S(2)}, u32[]{:S(2)}) collective-permute-start(bf16[256,320]{0,1:T(8,128)(2,1)S(1)} %get-tuple-element.8), channel_id=1, source_target_pairs={{4,0},{8,4},{12,8},{16,12},{20,16},{24,20},{28,24},{32,28},{36,32}... | collective-permute-start | bytes 491528 | tf_op jit(solution)/shard_map/ppermute | solution.py:10
  95.6 1.2 stack.4
  96.8 5.0 %all-to-all-start.2 = ((f32[4,256,320]{1,2,0:T(8,128)}), f32[4,256,320]{1,2,0:T(8,128)S(1)}, u32[]{:S(2)}, u32[]{:S(2)}) async-start(f32[4,256,320]{1,2,0:T(8,128)} %stack.4), calls=%async_computation.2 | async-start | bytes 2621440 | tf_op jit(solution)/shard_map/all_to_all | solution.py:134
  101.8 1.4 fusion.13
  104.3 1.6 copy.115
  107.9 1.3 gather_fusion.3
  110.3 1.3 gather_fusion.4
  112.7 1.3 gather_fusion.5
  115.0 1.3 gather_fusion.6
  117.3 1.3 gather_fusion.7
  124.8 1.3 gather_fusion.9
  126.3 1.6 fusion.66
  127.9 1.9 %collective-permute-start.2 = (bf16[256,320]{0,1:T(8,128)(2,1)S(1)}, bf16[256,320]{0,1:T(8,128)(2,1)S(1)}, u32[]{:S(2)}, u32[]{:S(2)}) collective-permute-start(bf16[256,320]{0,1:T(8,128)(2,1)S(1)} %get-tuple-element.27), channel_id=1, source_target_pairs={{508,0},{0,4},{4,8},{8,12},{12,16},{16,20},{20,24},{24,28},{28,32}... | collective-permute-start | bytes 491528 | tf_op jit(solution)/shard_map/ppermute | solution.py:10
  129.9 7.0 %collective-permute-start.3 = (bf16[256,320]{0,1:T(8,128)(2,1)S(1)}, bf16[256,320]{0,1:T(8,128)(2,1)S(1)}, u32[]{:S(2)}, u32[]{:S(2)}) collective-permute-start(bf16[256,320]{0,1:T(8,128)(2,1)S(1)} %get-tuple-element.27), channel_id=1, source_target_pairs={{4,0},{8,4},{12,8},{16,12},{20,16},{24,20},{28,24},{32,28},{36,32}... | collective-permute-start | bytes 491528 | tf_op jit(solution)/shard_map/ppermute | solution.py:10
  136.8 1.2 stack.5
  138.0 4.8 %all-to-all-start.3 = ((f32[4,256,320]{1,2,0:T(8,128)}), f32[4,256,320]{1,2,0:T(8,128)S(1)}, u32[]{:S(2)}, u32[]{:S(2)}) async-start(f32[4,256,320]{1,2,0:T(8,128)} %stack.5), calls=%async_computation.3 | async-start | bytes 2621440 | tf_op jit(solution)/shard_map/all_to_all | solution.py:134
  142.8 1.3 fusion.12
  145.3 1.6 copy.130
  146.8 1.9 %gather_fusion.14 = f32[256,320]{1,0:T(8,128)} fusion(f32[768,320]{1,0:T(8,128)S(1)} %copy.130, s32[1024]{0:T(1024)} %pad_clamp_fusion.3), kind=kCustom, calls=%fused_computation.11.clone | custom fusion | bytes 656384 | tf_op jit(solution)/shard_map/jit(_take)/gather | solution.py:38
  148.7 1.9 %gather_fusion.13 = f32[256,320]{1,0:T(8,128)} fusion(f32[768,320]{1,0:T(8,128)S(1)} %copy.130, s32[1024]{0:T(1024)} %pad_clamp_fusion.4), kind=kCustom, calls=%fused_computation.10.clone | custom fusion | bytes 656384 | tf_op jit(solution)/shard_map/jit(_take)/gather | solution.py:38
  150.6 1.9 %gather_fusion.12 = f32[256,320]{1,0:T(8,128)} fusion(f32[768,320]{1,0:T(8,128)S(1)} %copy.130, s32[1024]{0:T(1024)} %pad_clamp_fusion.5), kind=kCustom, calls=%fused_computation.9.clone | custom fusion | bytes 656384 | tf_op jit(solution)/shard_map/jit(_take)/gather | solution.py:38
  152.4 1.9 %gather_fusion.11 = f32[256,320]{1,0:T(8,128)} fusion(f32[768,320]{1,0:T(8,128)S(1)} %copy.130, s32[1024]{0:T(1024)} %pad_clamp_fusion.6), kind=kCustom, calls=%fused_computation.8.clone | custom fusion | bytes 656384 | tf_op jit(solution)/shard_map/jit(_take)/gather | solution.py:38
  167.9 1.3 fusion.7
  (219 shorter events, 41.6 us)
Async XLA Ops:
  0.0 101.8 %copy-start = (bf16[320,320]{1,0:T(8,128)(2,1)S(1)}, bf16[320,320]{1,0:T(8,128)(2,1)}, u32[]{:S(2)}) copy-start(bf16[320,320]{1,0:T(8,128)(2,1)} %param.19) | copy-start | bytes 614404
  0.0 25.1 %copy-start.41 = (s32[256]{0:T(256)S(1)}, s32[256]{0:T(256)}, u32[]{:S(2)}) copy-start(s32[256]{0:T(256)} %param.17) | copy-start | bytes 3076
  0.0 25.4 %copy-start.18 = (bf16[256,320]{0,1:T(8,128)(2,1)S(1)}, bf16[256,320]{0,1:T(8,128)(2,1)}, u32[]{:S(2)}) copy-start(bf16[256,320]{0,1:T(8,128)(2,1)} %param.15) | copy-start | bytes 491524
  5.2 22.9 %copy-start.19 = (s32[6,256]{1,0:T(8,128)S(1)}, s32[6,256]{1,0:T(8,128)}, u32[]{:S(2)}) copy-start(s32[6,256]{1,0:T(8,128)} %param.20) | copy-start | bytes 18436
  5.2 26.0 %copy-start.27 = (s32[2,256]{1,0:T(2,128)S(1)}, s32[2,256]{1,0:T(2,128)}, u32[]{:S(2)}) copy-start(s32[2,256]{1,0:T(2,128)} %param.22) | copy-start | bytes 6148
  5.2 45.5 %all-to-all-start.1 = ((bf16[128,4,320]{2,1,0:T(4,128)(2,1)}), bf16[128,4,320]{2,1,0:T(4,128)(2,1)S(1)}, u32[]{:S(2)}, u32[]{:S(2)}) async-start(bf16[128,4,320]{2,1,0:T(4,128)(2,1)} %reshape.193), calls=%async_computation.1 | async-start | bytes 786432 | tf_op jit(solution)/shard_map/all_to_all | solution.py:114
  25.4 35.6 %copy-start.28 = (f32[2,256]{1,0:T(2,128)S(1)}, f32[2,256]{1,0:T(2,128)}, u32[]{:S(2)}) copy-start(f32[2,256]{1,0:T(2,128)} %param.23) | copy-start | bytes 6148
  25.4 36.2 %copy-start.26 = (f32[6,256]{1,0:T(8,128)S(1)}, f32[6,256]{1,0:T(8,128)}, u32[]{:S(2)}) copy-start(f32[6,256]{1,0:T(8,128)} %param.21) | copy-start | bytes 18436
  28.2 77.7 %copy-start.25 = (s32[1024]{0:T(1024)}, s32[1024]{0:T(1024)S(1)}, u32[]{:S(2)}) copy-start(s32[1024]{0:T(1024)S(1)} %pad_clamp_fusion.7) | copy-start | bytes 12292
  31.3 92.3 %copy-start.24 = (s32[1024]{0:T(1024)}, s32[1024]{0:T(1024)S(1)}, u32[]{:S(2)}) copy-start(s32[1024]{0:T(1024)S(1)} %pad_clamp_fusion.1) | copy-start | bytes 12292
  50.8 34.3 %all-to-all-start = ((bf16[128,4,320]{2,1,0:T(4,128)(2,1)}), bf16[128,4,320]{2,1,0:T(4,128)(2,1)S(1)}, u32[]{:S(2)}, u32[]{:S(2)}) async-start(bf16[128,4,320]{2,1,0:T(4,128)(2,1)} %reshape.191), calls=%async_computation | async-start | bytes 786432 | tf_op jit(solution)/shard_map/all_to_all | solution.py:117
  61.7 58.3 %copy-start.20 = (f32[1,256]{1,0:T(1,128)}, f32[1,256]{1,0:T(1,128)S(1)}, u32[]{:S(2)}) copy-start(f32[1,256]{1,0:T(1,128)S(1)} %get-tuple-element.12) | copy-start | bytes 3076
  61.7 58.3 %copy-start.22 = (f32[1,256]{1,0:T(1,128)}, f32[1,256]{1,0:T(1,128)S(1)}, u32[]{:S(2)}) copy-start(f32[1,256]{1,0:T(1,128)S(1)} %get-tuple-element.11) | copy-start | bytes 3076
  63.2 38.6 %copy-start.4 = (bf16[256,320]{0,1:T(8,128)(2,1)}, bf16[256,320]{0,1:T(8,128)(2,1)S(1)}, u32[]{:S(2)}) copy-start(bf16[256,320]{0,1:T(8,128)(2,1)S(1)} %copy.114) | copy-start | bytes 491524
  86.6 15.2 %copy-start.7 = (bf16[256,320]{0,1:T(8,128)(2,1)}, bf16[256,320]{0,1:T(8,128)(2,1)S(1)}, u32[]{:S(2)}) copy-start(bf16[256,320]{0,1:T(8,128)(2,1)S(1)} %copy.112) | copy-start | bytes 491524
  86.7 16.5 %collective-permute-start = (bf16[256,320]{0,1:T(8,128)(2,1)S(1)}, bf16[256,320]{0,1:T(8,128)(2,1)S(1)}, u32[]{:S(2)}, u32[]{:S(2)}) collective-permute-start(bf16[256,320]{0,1:T(8,128)(2,1)S(1)} %get-tuple-element.8), channel_id=1, source_target_pairs={{508,0},{0,4},{4,8},{8,12},{12,16},{16,20},{20,24},{24,28},{28,32}... | collective-permute-start | bytes 491528 | tf_op jit(solution)/shard_map/ppermute | solution.py:10
  88.6 14.6 %collective-permute-start.1 = (bf16[256,320]{0,1:T(8,128)(2,1)S(1)}, bf16[256,320]{0,1:T(8,128)(2,1)S(1)}, u32[]{:S(2)}, u32[]{:S(2)}) collective-permute-start(bf16[256,320]{0,1:T(8,128)(2,1)S(1)} %get-tuple-element.8), channel_id=1, source_target_pairs={{4,0},{8,4},{12,8},{16,12},{20,16},{24,20},{28,24},{32,28},{36,32}... | collective-permute-start | bytes 491528 | tf_op jit(solution)/shard_map/ppermute | solution.py:10
  96.8 5.1 %copy-start.13 = (bf16[320,320]{1,0:T(8,128)(2,1)S(1)}, bf16[320,320]{1,0:T(8,128)(2,1)}, u32[]{:S(2)}) copy-start(bf16[320,320]{1,0:T(8,128)(2,1)} %param.18) | copy-start | bytes 614404
  96.8 26.3 %all-to-all-start.2 = ((f32[4,256,320]{1,2,0:T(8,128)}), f32[4,256,320]{1,2,0:T(8,128)S(1)}, u32[]{:S(2)}, u32[]{:S(2)}) async-start(f32[4,256,320]{1,2,0:T(8,128)} %stack.4), calls=%async_computation.2 | async-start | bytes 2621440 | tf_op jit(solution)/shard_map/all_to_all | solution.py:134
  124.7 1.5 copy-start.5
  124.7 1.5 copy-start.8
  124.8 1.5 copy-start.11
  124.8 1.5 copy-start.14
  124.8 1.5 copy-start.42
  124.8 1.5 copy-start.44
  124.8 1.5 copy-start.46
  127.9 14.9 %copy-start.16 = (bf16[256,320]{0,1:T(8,128)(2,1)}, bf16[256,320]{0,1:T(8,128)(2,1)S(1)}, u32[]{:S(2)}) copy-start(bf16[256,320]{0,1:T(8,128)(2,1)S(1)} %get-tuple-element.27) | copy-start | bytes 491524
  127.9 16.2 %collective-permute-start.2 = (bf16[256,320]{0,1:T(8,128)(2,1)S(1)}, bf16[256,320]{0,1:T(8,128)(2,1)S(1)}, u32[]{:S(2)}, u32[]{:S(2)}) collective-permute-start(bf16[256,320]{0,1:T(8,128)(2,1)S(1)} %get-tuple-element.27), channel_id=1, source_target_pairs={{508,0},{0,4},{4,8},{8,12},{12,16},{16,20},{20,24},{24,28},{28,32}... | collective-permute-start | bytes 491528 | tf_op jit(solution)/shard_map/ppermute | solution.py:10
  129.9 14.3 %collective-permute-start.3 = (bf16[256,320]{0,1:T(8,128)(2,1)S(1)}, bf16[256,320]{0,1:T(8,128)(2,1)S(1)}, u32[]{:S(2)}, u32[]{:S(2)}) collective-permute-start(bf16[256,320]{0,1:T(8,128)(2,1)S(1)} %get-tuple-element.27), channel_id=1, source_target_pairs={{4,0},{8,4},{12,8},{16,12},{20,16},{24,20},{28,24},{32,28},{36,32}... | collective-permute-start | bytes 491528 | tf_op jit(solution)/shard_map/ppermute | solution.py:10
  138.0 25.9 %all-to-all-start.3 = ((f32[4,256,320]{1,2,0:T(8,128)}), f32[4,256,320]{1,2,0:T(8,128)S(1)}, u32[]{:S(2)}, u32[]{:S(2)}) async-start(f32[4,256,320]{1,2,0:T(8,128)} %stack.5), calls=%async_computation.3 | async-start | bytes 2621440 | tf_op jit(solution)/shard_map/all_to_all | solution.py:134
  156.5 2.1 %copy-start.3 = (f32[256,320]{1,0:T(8,128)S(1)}, f32[256,320]{1,0:T(8,128)}, u32[]{:S(2)}) copy-start(f32[256,320]{1,0:T(8,128)} %gather_fusion.13) | copy-start | bytes 983044
  156.6 2.1 %copy-start.38 = (pred[256]{0:T(512)(128)(4,1)S(1)}, pred[256]{0:T(512)(128)(4,1)}, u32[]{:S(2)}) copy-start(pred[256]{0:T(512)(128)(4,1)} %compare_and_fusion.4) | copy-start | bytes 772
  (26 other events, 29.6 us)
